TPU v7x, 32 devices: a whole 2x2x4 slice. The times are simulated.
32 devices in a mesh: samples: 8 (over z, y), snps: 4 (over x, core).
Axes of the slice: x: 2, y: 2, z: 4, core: 2. Of those that a mesh axis runs over, the one named last changes fastest.
Arguments:
- genotype: int32 [4096, 1536], P('samples', 'snps'), may hold values from 0 to 2
- mask: int32 [4096, 1536], P('samples', 'snps'), may hold values 0 or 1
Outputs:
- blocks: float32 [4096, 2560], P('samples', 'snps')
All inputs are finite; a program needn't handle non-finite values. No bound on the sum of `mask` on one device may be relied on, other than what follows from the above.
Results may differ from a plain program's by a relative error of at most 0.0014.
Values may be sent and summed in bfloat16 or wider, within the bound.
A program may use at most 128 MiB of HBM per device.

v0:
```python
import math
import jax
import jax.numpy as jnp
from jax import lax
from jax.sharding import PartitionSpec as P


def standardize(dosage, observed_mask, allele_sum, observed_sum):
    frequency = (allele_sum + 1.0) / (2.0 * observed_sum + 2.0)
    scaled = (
        observed_mask * (dosage - 2.0 * frequency) / jnp.sqrt(2.0 * frequency * (1.0 - frequency))
    )
    return scaled.astype(jnp.bfloat16)


def cross_block(own_rows, other_rows):
    return lax.dot_general(
        own_rows, other_rows, (((1,), (1,)), ((), ())), preferred_element_type=jnp.float32
    )


def rows_for_columns(full_rows, offsets):
    circle_size = lax.axis_size("samples")
    parts = lax.axis_size("snps")
    block_rows = full_rows.shape[0]
    width = offsets * block_rows // parts
    piece = math.gcd(block_rows, width)
    per_block = block_rows // piece
    per_part = width // piece
    part = lax.axis_index("snps")
    pieces = []
    for index in range(per_part):
        sub = (part * per_part + index) % per_block
        sent = lax.dynamic_slice_in_dim(full_rows, sub * piece, piece, axis=0)
        pairs = []
        for row in range(circle_size):
            for column in range(parts):
                ahead = (column * per_part + index) // per_block
                source = (row + ahead) % circle_size
                pairs.append((source * parts + column, row * parts + column))
        pieces.append(lax.ppermute(sent, ("samples", "snps"), pairs))
    return jnp.concatenate(pieces, axis=0)


def per_device(genotype, mask):
    dosage = genotype.astype(jnp.float32)
    observed_mask = mask.astype(jnp.float32)
    allele_sum, observed_sum = lax.psum(
        (jnp.sum(dosage * observed_mask, axis=0), jnp.sum(observed_mask, axis=0)), "samples"
    )
    standard = standardize(dosage, observed_mask, allele_sum, observed_sum)
    offsets = lax.axis_size("samples") // 2 + 1
    full_rows = lax.all_gather(standard, "snps", axis=1, tiled=True)
    others = rows_for_columns(full_rows, offsets)
    return cross_block(full_rows, others) / full_rows.shape[1]


def solution(mesh):
    return jax.shard_map(
        per_device,
        mesh=mesh,
        in_specs=(P("samples", "snps"), P("samples", "snps")),
        out_specs=P("samples", "snps"),
        check_vma=False,
    )
```

profile of v0, /device:TPU:3, one launch (start us, length us, event | category | flops | bytes accessed | tf_op | source)
XLA Modules:
  0.0 140.2 jit_solution(2090311282719203152)
XLA Ops:
  6.5 0.0 copy-start.1
  6.5 0.0 copy-start
  6.5 0.0 all-gather.2.cloned.1.call-start
  6.5 1.6 %multiply_reduce_fusion = (f32[384]{0:T(512)S(1)}, f32[384]{0:T(512)S(1)}) fusion(s32[512,384]{1,0:T(8,128)} %param.2, s32[512,384]{1,0:T(8,128)} %param.3), kind=kLoop, calls=%fused_computation.2 | loop fusion | flops 982272 | bytes 1575936 | tf_op jit(solution)/shard_map/reduce_sum | solution.py:49
  8.2 17.9 %all-reduce = (f32[384]{0:T(512)S(1)}, f32[384]{0:T(512)S(1)}) all-reduce(f32[384]{0:T(512)S(1)} %get-tuple-element.6, f32[384]{0:T(512)S(1)} %get-tuple-element.5), channel_id=1, replica_groups=mesh['samples'=8,'snps'=4] {'samples'}, use_global_device_ids=true, to_apply=%region_3.0 | all-reduce | flops 768 | bytes 6144 | tf_op jit(solution)/shard_map/psum | solution.py:48
  26.1 0.0 copy-done.1
  26.1 0.0 copy-done
  26.1 0.9 divide_convert_fusion
  27.0 0.0 all-gather.2.cloned.1.call-update
  27.1 20.0 %all-gather.2.cloned.1.call-done = bf16[512,1536]{1,0:T(8,128)(2,1)} async-done(((bf16[512,384]{1,0:T(8,128)(2,1)}), bf16[512,1536]{1,0:T(8,128)(2,1)}) %all-gather.2.cloned.1.call-update) | async-done | bytes 1572880 | tf_op jit(solution)/shard_map/all_gather | solution.py:53
  47.1 1.6 %constant_dynamic-slice_fusion = (bf16[128,1536]{1,0:T(8,128)(2,1)S(1)}, bf16[128,1536]{1,0:T(8,128)(2,1)S(1)}, bf16[128,1536]{1,0:T(8,128)(2,1)S(1)}, bf16[128,1536]{1,0:T(8,128)(2,1)S(1)}, bf16[128,1536]{1,0:T(8,128)(2,1)S(1)}) fusion(bf16[512,1536]{1,0:T(8,128)(2,1)} %all-gather.2.cloned.1.call-done, s32[]{:T(128)S(6)} %select_n.47, s32[]{:T(128)S(6)} %select_n.45, ...), kind=kLoop, calls=%fused_computation.11 | loop fusion | bytes 3932180 | tf_op jit(solution)/shard_map/dynamic_slice | solution.py:34
  48.7 5.2 %collective-permute-start = (bf16[128,1536]{1,0:T(8,128)(2,1)S(1)}, bf16[128,1536]{1,0:T(8,128)(2,1)S(1)}, u32[]{:S(2)}, u32[]{:S(2)}) collective-permute-start(bf16[128,1536]{1,0:T(8,128)(2,1)S(1)} %get-tuple-element.15), channel_id=1, source_target_pairs={{0,0},{5,1},{10,2},{15,3},{4,4},{9,5},{14,6},{19,7},{8,8},{13,9},{... | collective-permute-start | bytes 1179656 | tf_op jit(solution)/shard_map/ppermute | solution.py:41
  53.9 2.1 %collective-permute-start.1 = (bf16[128,1536]{1,0:T(8,128)(2,1)S(1)}, bf16[128,1536]{1,0:T(8,128)(2,1)S(1)}, u32[]{:S(2)}, u32[]{:S(2)}) collective-permute-start(bf16[128,1536]{1,0:T(8,128)(2,1)S(1)} %get-tuple-element.14), channel_id=1, source_target_pairs={{0,0},{5,1},{10,2},{19,3},{4,4},{9,5},{14,6},{23,7},{8,8},{13,9},{... | collective-permute-start | bytes 1179656 | tf_op jit(solution)/shard_map/ppermute | solution.py:41
  56.0 2.2 %collective-permute-start.4 = (bf16[128,1536]{1,0:T(8,128)(2,1)S(1)}, bf16[128,1536]{1,0:T(8,128)(2,1)S(1)}, u32[]{:S(2)}, u32[]{:S(2)}) collective-permute-start(bf16[128,1536]{1,0:T(8,128)(2,1)S(1)} %get-tuple-element.11), channel_id=1, source_target_pairs={{4,0},{9,1},{14,2},{19,3},{8,4},{13,5},{18,6},{23,7},{12,8},{17,9}... | collective-permute-start | bytes 1179656 | tf_op jit(solution)/shard_map/ppermute | solution.py:41
  58.2 2.1 %collective-permute-start.3 = (bf16[128,1536]{1,0:T(8,128)(2,1)S(1)}, bf16[128,1536]{1,0:T(8,128)(2,1)S(1)}, u32[]{:S(2)}, u32[]{:S(2)}) collective-permute-start(bf16[128,1536]{1,0:T(8,128)(2,1)S(1)} %get-tuple-element.12), channel_id=1, source_target_pairs={{0,0},{9,1},{14,2},{19,3},{4,4},{13,5},{18,6},{23,7},{8,8},{17,9},... | collective-permute-start | bytes 1179656 | tf_op jit(solution)/shard_map/ppermute | solution.py:41
  60.3 0.0 copy-start.2
  60.3 4.2 %collective-permute-start.2 = (bf16[128,1536]{1,0:T(8,128)(2,1)S(1)}, bf16[128,1536]{1,0:T(8,128)(2,1)S(1)}, u32[]{:S(2)}, u32[]{:S(2)}) collective-permute-start(bf16[128,1536]{1,0:T(8,128)(2,1)S(1)} %get-tuple-element.13), channel_id=1, source_target_pairs={{0,0},{5,1},{14,2},{19,3},{4,4},{9,5},{18,6},{23,7},{8,8},{13,9},{... | collective-permute-start | bytes 1179656 | tf_op jit(solution)/shard_map/ppermute | solution.py:41
  64.5 0.0 collective-permute-done
  64.6 41.0 %collective-permute-done.1 = bf16[128,1536]{1,0:T(8,128)(2,1)S(1)} collective-permute-done((bf16[128,1536]{1,0:T(8,128)(2,1)S(1)}, bf16[128,1536]{1,0:T(8,128)(2,1)S(1)}, u32[]{:S(2)}, u32[]{:S(2)}) %collective-permute-start.1) | collective-permute-done | bytes 393248 | tf_op jit(solution)/shard_map/ppermute | solution.py:41
  105.6 25.1 %collective-permute-done.2 = bf16[128,1536]{1,0:T(8,128)(2,1)S(1)} collective-permute-done((bf16[128,1536]{1,0:T(8,128)(2,1)S(1)}, bf16[128,1536]{1,0:T(8,128)(2,1)S(1)}, u32[]{:S(2)}, u32[]{:S(2)}) %collective-permute-start.2) | collective-permute-done | bytes 393248 | tf_op jit(solution)/shard_map/ppermute | solution.py:41
  130.7 0.0 collective-permute-done.3
  130.8 0.0 collective-permute-done.4
  130.8 0.0 copy-done.2
  130.8 2.5 %convolution_multiply_fusion = f32[512,640]{1,0:T(8,128)} fusion(bf16[512,1536]{1,0:T(8,128)(2,1)S(1)} %copy-done.2, bf16[640,1536]{1,0:T(8,128)(2,1)S(1)} %constant_dynamic-update-slice_fusion), kind=kOutput, calls=%fused_computation | convolution fusion | flops 1006960640 | bytes 4849664 | tf_op jit(solution)/shard_map/dot_general | solution.py:17
  (7 shorter events, 0.2 us)
Async XLA Ops:
  6.5 19.6 %copy-start.1 = (s32[512,384]{1,0:T(8,128)S(1)}, s32[512,384]{1,0:T(8,128)}, u32[]{:S(2)}) copy-start(s32[512,384]{1,0:T(8,128)} %param.3) | copy-start | bytes 2359300
  6.5 19.6 %copy-start = (s32[512,384]{1,0:T(8,128)S(1)}, s32[512,384]{1,0:T(8,128)}, u32[]{:S(2)}) copy-start(s32[512,384]{1,0:T(8,128)} %param.2) | copy-start | bytes 2359300
  6.5 40.6 %all-gather.2.cloned.1.call-start = ((), (), s32[]{:S(2)}) async-start(), calls=%async_computation | async-start | bytes 1966080 | tf_op jit(solution)/shard_map/all_gather | solution.py:53
  48.7 15.8 %collective-permute-start = (bf16[128,1536]{1,0:T(8,128)(2,1)S(1)}, bf16[128,1536]{1,0:T(8,128)(2,1)S(1)}, u32[]{:S(2)}, u32[]{:S(2)}) collective-permute-start(bf16[128,1536]{1,0:T(8,128)(2,1)S(1)} %get-tuple-element.15), channel_id=1, source_target_pairs={{0,0},{5,1},{10,2},{15,3},{4,4},{9,5},{14,6},{19,7},{8,8},{13,9},{... | collective-permute-start | bytes 1179656 | tf_op jit(solution)/shard_map/ppermute | solution.py:41
  53.9 51.7 %collective-permute-start.1 = (bf16[128,1536]{1,0:T(8,128)(2,1)S(1)}, bf16[128,1536]{1,0:T(8,128)(2,1)S(1)}, u32[]{:S(2)}, u32[]{:S(2)}) collective-permute-start(bf16[128,1536]{1,0:T(8,128)(2,1)S(1)} %get-tuple-element.14), channel_id=1, source_target_pairs={{0,0},{5,1},{10,2},{19,3},{4,4},{9,5},{14,6},{23,7},{8,8},{13,9},{... | collective-permute-start | bytes 1179656 | tf_op jit(solution)/shard_map/ppermute | solution.py:41
  56.0 74.8 %collective-permute-start.4 = (bf16[128,1536]{1,0:T(8,128)(2,1)S(1)}, bf16[128,1536]{1,0:T(8,128)(2,1)S(1)}, u32[]{:S(2)}, u32[]{:S(2)}) collective-permute-start(bf16[128,1536]{1,0:T(8,128)(2,1)S(1)} %get-tuple-element.11), channel_id=1, source_target_pairs={{4,0},{9,1},{14,2},{19,3},{8,4},{13,5},{18,6},{23,7},{12,8},{17,9}... | collective-permute-start | bytes 1179656 | tf_op jit(solution)/shard_map/ppermute | solution.py:41
  58.2 72.6 %collective-permute-start.3 = (bf16[128,1536]{1,0:T(8,128)(2,1)S(1)}, bf16[128,1536]{1,0:T(8,128)(2,1)S(1)}, u32[]{:S(2)}, u32[]{:S(2)}) collective-permute-start(bf16[128,1536]{1,0:T(8,128)(2,1)S(1)} %get-tuple-element.12), channel_id=1, source_target_pairs={{0,0},{9,1},{14,2},{19,3},{4,4},{13,5},{18,6},{23,7},{8,8},{17,9},... | collective-permute-start | bytes 1179656 | tf_op jit(solution)/shard_map/ppermute | solution.py:41
  60.3 70.5 %copy-start.2 = (bf16[512,1536]{1,0:T(8,128)(2,1)S(1)}, bf16[512,1536]{1,0:T(8,128)(2,1)}, u32[]{:S(2)}) copy-start(bf16[512,1536]{1,0:T(8,128)(2,1)} %all-gather.2.cloned.1.call-done) | copy-start | bytes 4718596
  60.3 70.4 %collective-permute-start.2 = (bf16[128,1536]{1,0:T(8,128)(2,1)S(1)}, bf16[128,1536]{1,0:T(8,128)(2,1)S(1)}, u32[]{:S(2)}, u32[]{:S(2)}) collective-permute-start(bf16[128,1536]{1,0:T(8,128)(2,1)S(1)} %get-tuple-element.13), channel_id=1, source_target_pairs={{0,0},{5,1},{14,2},{19,3},{4,4},{9,5},{18,6},{23,7},{8,8},{13,9},{... | collective-permute-start | bytes 1179656 | tf_op jit(solution)/shard_map/ppermute | solution.py:41
Sparse Core Ops, SparseCore 0:
  27.2 19.8 all-gather.1
where the time goes:
time: 140 us
  waiting for transfers between devices  86.1 us (62%)
  blocking collectives  17.9 us (13%)
  starting transfers between devices  15.8 us (11%)
  between operations  13.6 us (10%)
  other arithmetic  2.56 us (2%)
  matrix products  2.47 us (2%)
  local copies, waits for them, and re-layouts  1.74 us (1%)
    ppermute x5, waiting for transfers between devices, rows_for_columns(): pieces.append(lax.ppermute(sent, ('samples', 'snps'), pairs))  66.1 us
    all_gather x1, waiting for transfers between devices, per_device(): full_rows = lax.all_gather(standard, 'snps', axis=1, tiled=True)  20 us
    psum x1, blocking collectives, per_device(): lax.psum((jnp.sum(dosage * observed_mask, axis=0), jnp.sum(observed_mask,...  17.9 us
    ppermute x5, starting transfers between devices, rows_for_columns(): pieces.append(lax.ppermute(sent, ('samples', 'snps'), pairs))  15.8 us
  transfers between devices with their start and end apart: 6, of which 3 were waited for; matrix products, arithmetic and copies ran while one was open for 0% of the time, Pallas kernels for 0%

commit v1 on v0

--- a/solution.py
+++ b/solution.py
@@ -3,6 +3,16 @@
 import jax.numpy as jnp
 from jax import lax
 from jax.sharding import PartitionSpec as P
+
+
+def gather_by_hops(x, mesh_axis, dim):
+    size = lax.axis_size(mesh_axis)
+    moving, blocks = (x, [x])
+    for _ in range(size - 1):
+        moving = lax.ppermute(moving, mesh_axis, [(i, (i + 1) % size) for i in range(size)])
+        blocks.insert(0, moving)
+    row_of_blocks = jnp.concatenate(blocks, axis=dim)
+    return jnp.roll(row_of_blocks, (lax.axis_index(mesh_axis) + 1) * x.shape[dim], axis=dim)
 
 
 def standardize(dosage, observed_mask, allele_sum, observed_sum):
@@ -50,7 +60,7 @@
     )
     standard = standardize(dosage, observed_mask, allele_sum, observed_sum)
     offsets = lax.axis_size("samples") // 2 + 1
-    full_rows = lax.all_gather(standard, "snps", axis=1, tiled=True)
+    full_rows = gather_by_hops(standard, "snps", 1)
     others = rows_for_columns(full_rows, offsets)
     return cross_block(full_rows, others) / full_rows.shape[1]
 

time: 140 us -> 127 us (0.907)
  between operations: 13.6 us -> 0.15 us
  waiting for transfers between devices: 86.1 us -> 78.1 us
  starting transfers between devices: 15.8 us -> 22 us
    all_gather x1 -> x0, waiting for transfers between devices: 20 us -> none  [per_device(): full_rows = lax.all_gather(standard, 'snps', axis=1, tiled=True)]
    ppermute x0 -> x3, waiting for transfers between devices: none -> 14.2 us  [gather_by_hops(): lax.ppermute(moving, mesh_axis, [(i, (i + 1) % size) for i in range(size)])]
    ppermute x0 -> x3, starting transfers between devices: none -> 9.58 us  [gather_by_hops(): lax.ppermute(moving, mesh_axis, [(i, (i + 1) % size) for i in range(size)])]
    ppermute x5, starting transfers between devices: 15.8 us -> 12.4 us  [rows_for_columns(): pieces.append(lax.ppermute(sent, ('samples', 'snps'), pairs))]
    ppermute x5, waiting for transfers between devices: 66.1 us -> 64 us  [rows_for_columns(): pieces.append(lax.ppermute(sent, ('samples', 'snps'), pairs))]
  transfers between devices with their start and end apart: 6 -> 8, of which waited for: 3 -> 6; matrix products, arithmetic and copies ran while one was open for 0% -> 0% of each run, Pallas kernels for 0% -> 0%
where the time goes in v1:
time: 127 us; the launch traced here: 126 us
  waiting for transfers between devices  78.1 us (61%)
  starting transfers between devices  22 us (17%)
  blocking collectives  17.9 us (14%)
  other arithmetic  3.08 us (2%)
  matrix products  2.54 us (2%)
  local copies, waits for them, and re-layouts  2.03 us (2%)
    ppermute x5, waiting for transfers between devices, rows_for_columns(): pieces.append(lax.ppermute(sent, ('samples', 'snps'), pairs))  64 us
    psum x1, blocking collectives, per_device(): lax.psum((jnp.sum(dosage * observed_mask, axis=0), jnp.sum(observed_mask,...  17.9 us
    ppermute x3, waiting for transfers between devices, gather_by_hops(): lax.ppermute(moving, mesh_axis, [(i, (i + 1) % size) for i in range(size)])  14.2 us
    ppermute x5, starting transfers between devices, rows_for_columns(): pieces.append(lax.ppermute(sent, ('samples', 'snps'), pairs))  12.4 us
    ppermute x3, starting transfers between devices, gather_by_hops(): lax.ppermute(moving, mesh_axis, [(i, (i + 1) % size) for i in range(size)])  9.58 us
    dot_general x1, matrix products, cross_block(): lax.dot_general(own_rows, other_rows, (((1,), (1,)), ((), ())), preferred...  2.54 us
  transfers between devices with their start and end apart: 8, of which 6 were waited for; matrix products, arithmetic and copies ran while one was open for 0% of the time, Pallas kernels for 0%

profile of v1, /device:TPU:3, one launch (start us, length us, event | category | flops | bytes accessed | tf_op | source)
XLA Modules:
  0.0 125.8 jit_solution(12144615645415700399)
XLA Ops:
  0.0 1.5 %multiply_reduce_fusion = (f32[384]{0:T(512)S(1)}, f32[384]{0:T(512)S(1)}) fusion(s32[512,384]{1,0:T(8,128)} %param.2, s32[512,384]{1,0:T(8,128)} %param.3), kind=kLoop, calls=%fused_computation.4 | loop fusion | flops 982272 | bytes 1575936 | tf_op jit(solution)/shard_map/reduce_sum | solution.py:59
  1.5 17.9 %all-reduce = (f32[384]{0:T(512)S(1)}, f32[384]{0:T(512)S(1)}) all-reduce(f32[384]{0:T(512)S(1)} %get-tuple-element.6, f32[384]{0:T(512)S(1)} %get-tuple-element.5), channel_id=1, replica_groups=mesh['samples'=8,'snps'=4] {'samples'}, use_global_device_ids=true, to_apply=%region_3.0 | all-reduce | flops 768 | bytes 6144 | tf_op jit(solution)/shard_map/psum | solution.py:58
  19.5 1.5 %divide_convert_fusion = bf16[512,384]{1,0:T(8,128)(2,1)S(1)} fusion(s32[512,384]{1,0:T(8,128)} %param.2, s32[512,384]{1,0:T(8,128)} %param.3, f32[384]{0:T(512)S(1)} %multiply_sqrt_fusion, f32[384]{0:T(512)S(1)} %get-tuple-element.9), kind=kLoop, calls=%fused_computation.3 | loop fusion | flops 1179648 | bytes 1969152 | tf_op jit(solution)/shard_map/convert_element_type | solution.py:23
  21.0 4.6 %collective-permute-start = (bf16[512,384]{1,0:T(8,128)(2,1)S(1)}, bf16[512,384]{1,0:T(8,128)(2,1)S(1)}, u32[]{:S(2)}, u32[]{:S(2)}) collective-permute-start(bf16[512,384]{1,0:T(8,128)(2,1)S(1)} %divide_convert_fusion), channel_id=1, source_target_pairs={{0,1},{1,2},{2,3},{3,0},{4,5},{5,6},{6,7},{7,4},{8,9},{9,10},{10,1... | collective-permute-start | bytes 1179656 | tf_op jit(solution)/shard_map/ppermute | solution.py:12
  25.6 4.7 %collective-permute-done = bf16[512,384]{1,0:T(8,128)(2,1)S(1)} collective-permute-done((bf16[512,384]{1,0:T(8,128)(2,1)S(1)}, bf16[512,384]{1,0:T(8,128)(2,1)S(1)}, u32[]{:S(2)}, u32[]{:S(2)}) %collective-permute-start) | collective-permute-done | bytes 393248 | tf_op jit(solution)/shard_map/ppermute | solution.py:12
  30.3 2.5 %collective-permute-start.1 = (bf16[512,384]{1,0:T(8,128)(2,1)S(1)}, bf16[512,384]{1,0:T(8,128)(2,1)S(1)}, u32[]{:S(2)}, u32[]{:S(2)}) collective-permute-start(bf16[512,384]{1,0:T(8,128)(2,1)S(1)} %collective-permute-done), channel_id=1, source_target_pairs={{0,1},{1,2},{2,3},{3,0},{4,5},{5,6},{6,7},{7,4},{8,9},{9,10},{10,1... | collective-permute-start | bytes 1179656 | tf_op jit(solution)/shard_map/ppermute | solution.py:12
  32.8 4.7 %collective-permute-done.1 = bf16[512,384]{1,0:T(8,128)(2,1)S(1)} collective-permute-done((bf16[512,384]{1,0:T(8,128)(2,1)S(1)}, bf16[512,384]{1,0:T(8,128)(2,1)S(1)}, u32[]{:S(2)}, u32[]{:S(2)}) %collective-permute-start.1) | collective-permute-done | bytes 393248 | tf_op jit(solution)/shard_map/ppermute | solution.py:12
  37.6 2.5 %collective-permute-start.2 = (bf16[512,384]{1,0:T(8,128)(2,1)S(1)}, bf16[512,384]{1,0:T(8,128)(2,1)S(1)}, u32[]{:S(2)}, u32[]{:S(2)}) collective-permute-start(bf16[512,384]{1,0:T(8,128)(2,1)S(1)} %collective-permute-done.1), channel_id=1, source_target_pairs={{0,1},{1,2},{2,3},{3,0},{4,5},{5,6},{6,7},{7,4},{8,9},{9,10},{10,1... | collective-permute-start | bytes 1179656 | tf_op jit(solution)/shard_map/ppermute | solution.py:12
  40.0 4.7 %collective-permute-done.2 = bf16[512,384]{1,0:T(8,128)(2,1)S(1)} collective-permute-done((bf16[512,384]{1,0:T(8,128)(2,1)S(1)}, bf16[512,384]{1,0:T(8,128)(2,1)S(1)}, u32[]{:S(2)}, u32[]{:S(2)}) %collective-permute-start.2) | collective-permute-done | bytes 393248 | tf_op jit(solution)/shard_map/ppermute | solution.py:12
  44.8 0.1 constant_dynamic-update-slice_fusion.7
  44.8 0.1 constant_dynamic-update-slice_fusion.6
  44.9 0.1 constant_dynamic-update-slice_fusion.5
  45.0 0.1 constant_dynamic-update-slice_fusion.4
  45.1 0.1 constant_dynamic-update-slice_fusion.3
  45.2 0.1 constant_dynamic-update-slice_fusion.2
  45.3 0.1 constant_dynamic-update-slice_fusion.1
  45.4 0.1 constant_dynamic-update-slice_fusion
  45.5 1.2 fusion.6
  46.7 1.9 %collective-permute-start.3 = (bf16[128,1536]{1,0:T(8,128)(2,1)S(1)}, bf16[128,1536]{1,0:T(8,128)(2,1)S(1)}, u32[]{:S(2)}, u32[]{:S(2)}) collective-permute-start(bf16[128,1536]{1,0:T(8,128)(2,1)S(1)} %get-tuple-element.15), channel_id=1, source_target_pairs={{0,0},{5,1},{10,2},{15,3},{4,4},{9,5},{14,6},{19,7},{8,8},{13,9},{... | collective-permute-start | bytes 1179656 | tf_op jit(solution)/shard_map/ppermute | solution.py:51
  48.6 1.9 %collective-permute-start.4 = (bf16[128,1536]{1,0:T(8,128)(2,1)S(1)}, bf16[128,1536]{1,0:T(8,128)(2,1)S(1)}, u32[]{:S(2)}, u32[]{:S(2)}) collective-permute-start(bf16[128,1536]{1,0:T(8,128)(2,1)S(1)} %get-tuple-element.14), channel_id=1, source_target_pairs={{0,0},{5,1},{10,2},{19,3},{4,4},{9,5},{14,6},{23,7},{8,8},{13,9},{... | collective-permute-start | bytes 1179656 | tf_op jit(solution)/shard_map/ppermute | solution.py:51
  50.6 2.4 %collective-permute-start.7 = (bf16[128,1536]{1,0:T(8,128)(2,1)S(1)}, bf16[128,1536]{1,0:T(8,128)(2,1)S(1)}, u32[]{:S(2)}, u32[]{:S(2)}) collective-permute-start(bf16[128,1536]{1,0:T(8,128)(2,1)S(1)} %get-tuple-element.11), channel_id=1, source_target_pairs={{4,0},{9,1},{14,2},{19,3},{8,4},{13,5},{18,6},{23,7},{12,8},{17,9}... | collective-permute-start | bytes 1179656 | tf_op jit(solution)/shard_map/ppermute | solution.py:51
  53.0 1.9 %collective-permute-start.6 = (bf16[128,1536]{1,0:T(8,128)(2,1)S(1)}, bf16[128,1536]{1,0:T(8,128)(2,1)S(1)}, u32[]{:S(2)}, u32[]{:S(2)}) collective-permute-start(bf16[128,1536]{1,0:T(8,128)(2,1)S(1)} %get-tuple-element.12), channel_id=1, source_target_pairs={{0,0},{9,1},{14,2},{19,3},{4,4},{13,5},{18,6},{23,7},{8,8},{17,9},... | collective-permute-start | bytes 1179656 | tf_op jit(solution)/shard_map/ppermute | solution.py:51
  54.9 4.2 %collective-permute-start.5 = (bf16[128,1536]{1,0:T(8,128)(2,1)S(1)}, bf16[128,1536]{1,0:T(8,128)(2,1)S(1)}, u32[]{:S(2)}, u32[]{:S(2)}) collective-permute-start(bf16[128,1536]{1,0:T(8,128)(2,1)S(1)} %get-tuple-element.13), channel_id=1, source_target_pairs={{0,0},{5,1},{14,2},{19,3},{4,4},{9,5},{18,6},{23,7},{8,8},{13,9},{... | collective-permute-start | bytes 1179656 | tf_op jit(solution)/shard_map/ppermute | solution.py:51
  59.2 1.2 collective-permute-done.3
  60.4 37.5 %collective-permute-done.4 = bf16[128,1536]{1,0:T(8,128)(2,1)S(1)} collective-permute-done((bf16[128,1536]{1,0:T(8,128)(2,1)S(1)}, bf16[128,1536]{1,0:T(8,128)(2,1)S(1)}, u32[]{:S(2)}, u32[]{:S(2)}) %collective-permute-start.4) | collective-permute-done | bytes 393248 | tf_op jit(solution)/shard_map/ppermute | solution.py:51
  97.9 25.2 %collective-permute-done.5 = bf16[128,1536]{1,0:T(8,128)(2,1)S(1)} collective-permute-done((bf16[128,1536]{1,0:T(8,128)(2,1)S(1)}, bf16[128,1536]{1,0:T(8,128)(2,1)S(1)}, u32[]{:S(2)}, u32[]{:S(2)}) %collective-permute-start.5) | collective-permute-done | bytes 393248 | tf_op jit(solution)/shard_map/ppermute | solution.py:51
  123.2 0.0 collective-permute-done.6
  123.3 0.0 collective-permute-done.7
  123.3 2.5 %fusion.2 = f32[512,640]{1,0:T(8,128)} fusion(bf16[640,1536]{1,0:T(8,128)(2,1)S(1)} %constant_dynamic-update-slice_fusion.8, bf16[512,3072]{1,0:T(8,128)(2,1)S(1)} %constant_dynamic-update-slice_fusion, s32[]{:T(128)S(6)} %select_n.63), kind=kOutput, calls=%fused_computation.2 | convolution fusion | flops 1006960640 | bytes 4849668 | tf_op jit(solution)/shard_map/dot_general | solution.py:27
  (7 shorter events, 0.2 us)
Async XLA Ops:
  21.0 9.3 %collective-permute-start = (bf16[512,384]{1,0:T(8,128)(2,1)S(1)}, bf16[512,384]{1,0:T(8,128)(2,1)S(1)}, u32[]{:S(2)}, u32[]{:S(2)}) collective-permute-start(bf16[512,384]{1,0:T(8,128)(2,1)S(1)} %divide_convert_fusion), channel_id=1, source_target_pairs={{0,1},{1,2},{2,3},{3,0},{4,5},{5,6},{6,7},{7,4},{8,9},{9,10},{10,1... | collective-permute-start | bytes 1179656 | tf_op jit(solution)/shard_map/ppermute | solution.py:12
  30.3 7.2 %collective-permute-start.1 = (bf16[512,384]{1,0:T(8,128)(2,1)S(1)}, bf16[512,384]{1,0:T(8,128)(2,1)S(1)}, u32[]{:S(2)}, u32[]{:S(2)}) collective-permute-start(bf16[512,384]{1,0:T(8,128)(2,1)S(1)} %collective-permute-done), channel_id=1, source_target_pairs={{0,1},{1,2},{2,3},{3,0},{4,5},{5,6},{6,7},{7,4},{8,9},{9,10},{10,1... | collective-permute-start | bytes 1179656 | tf_op jit(solution)/shard_map/ppermute | solution.py:12
  37.6 7.2 %collective-permute-start.2 = (bf16[512,384]{1,0:T(8,128)(2,1)S(1)}, bf16[512,384]{1,0:T(8,128)(2,1)S(1)}, u32[]{:S(2)}, u32[]{:S(2)}) collective-permute-start(bf16[512,384]{1,0:T(8,128)(2,1)S(1)} %collective-permute-done.1), channel_id=1, source_target_pairs={{0,1},{1,2},{2,3},{3,0},{4,5},{5,6},{6,7},{7,4},{8,9},{9,10},{10,1... | collective-permute-start | bytes 1179656 | tf_op jit(solution)/shard_map/ppermute | solution.py:12
  46.7 13.6 %collective-permute-start.3 = (bf16[128,1536]{1,0:T(8,128)(2,1)S(1)}, bf16[128,1536]{1,0:T(8,128)(2,1)S(1)}, u32[]{:S(2)}, u32[]{:S(2)}) collective-permute-start(bf16[128,1536]{1,0:T(8,128)(2,1)S(1)} %get-tuple-element.15), channel_id=1, source_target_pairs={{0,0},{5,1},{10,2},{15,3},{4,4},{9,5},{14,6},{19,7},{8,8},{13,9},{... | collective-permute-start | bytes 1179656 | tf_op jit(solution)/shard_map/ppermute | solution.py:51
  48.6 49.2 %collective-permute-start.4 = (bf16[128,1536]{1,0:T(8,128)(2,1)S(1)}, bf16[128,1536]{1,0:T(8,128)(2,1)S(1)}, u32[]{:S(2)}, u32[]{:S(2)}) collective-permute-start(bf16[128,1536]{1,0:T(8,128)(2,1)S(1)} %get-tuple-element.14), channel_id=1, source_target_pairs={{0,0},{5,1},{10,2},{19,3},{4,4},{9,5},{14,6},{23,7},{8,8},{13,9},{... | collective-permute-start | bytes 1179656 | tf_op jit(solution)/shard_map/ppermute | solution.py:51
  50.6 72.7 %collective-permute-start.7 = (bf16[128,1536]{1,0:T(8,128)(2,1)S(1)}, bf16[128,1536]{1,0:T(8,128)(2,1)S(1)}, u32[]{:S(2)}, u32[]{:S(2)}) collective-permute-start(bf16[128,1536]{1,0:T(8,128)(2,1)S(1)} %get-tuple-element.11), channel_id=1, source_target_pairs={{4,0},{9,1},{14,2},{19,3},{8,4},{13,5},{18,6},{23,7},{12,8},{17,9}... | collective-permute-start | bytes 1179656 | tf_op jit(solution)/shard_map/ppermute | solution.py:51
  53.0 70.2 %collective-permute-start.6 = (bf16[128,1536]{1,0:T(8,128)(2,1)S(1)}, bf16[128,1536]{1,0:T(8,128)(2,1)S(1)}, u32[]{:S(2)}, u32[]{:S(2)}) collective-permute-start(bf16[128,1536]{1,0:T(8,128)(2,1)S(1)} %get-tuple-element.12), channel_id=1, source_target_pairs={{0,0},{9,1},{14,2},{19,3},{4,4},{13,5},{18,6},{23,7},{8,8},{17,9},... | collective-permute-start | bytes 1179656 | tf_op jit(solution)/shard_map/ppermute | solution.py:51
  54.9 68.3 %collective-permute-start.5 = (bf16[128,1536]{1,0:T(8,128)(2,1)S(1)}, bf16[128,1536]{1,0:T(8,128)(2,1)S(1)}, u32[]{:S(2)}, u32[]{:S(2)}) collective-permute-start(bf16[128,1536]{1,0:T(8,128)(2,1)S(1)} %get-tuple-element.13), channel_id=1, source_target_pairs={{0,0},{5,1},{14,2},{19,3},{4,4},{9,5},{18,6},{23,7},{8,8},{13,9},{... | collective-permute-start | bytes 1179656 | tf_op jit(solution)/shard_map/ppermute | solution.py:51
